TPU v7x, 32 devices: a whole 2x2x4 slice. The times are simulated.
32 devices in a mesh: dp: 8 (over z, x), latent: 4 (over y, core).
Axes of the slice: x: 2, y: 2, z: 4, core: 2. Of those that a mesh axis runs over, the one named last changes fastest.
Arguments:
- tokens: bfloat16 [1024, 1536], P('dp'), may hold values from -6 to 6
- enc_weight: bfloat16 [1536, 32768], P(None, ('dp', 'latent')), may hold values from -0.15625 to 0.15625
- enc_bias: float32 [32768], P(('dp', 'latent')), may hold values from -3 to 3
- dec_weight: bfloat16 [32768, 1536], P(('dp', 'latent')), may hold values from -0.0625 to 0.0625
- dec_bias: float32 [1536], replicated, may hold values from -3 to 3
- slot_token: int32 [1024], P(('dp', 'latent')), may hold values from 0 to 7
- slot_latent: int32 [1024], P(('dp', 'latent')), may hold values from 0 to 7
- slot_count: int32 [32], P(('dp', 'latent')), may hold values from 6 to 32, as said below
Outputs:
- enc_grad: bfloat16 [1536, 32768], P(None, ('dp', 'latent'))
- dec_grad: bfloat16 [32768, 1536], P(('dp', 'latent'))
- enc_bias_grad: float32 [32768], P(('dp', 'latent'))
- dec_bias_grad: float32 [1536], replicated
- mean_error: float32 [], replicated
Inputs may be any that keep to these rules, and one draw needn't show every extreme that they name: `slot_count`: slot lists of one device never repeat a (token block, latent block) pair among its 32 slots; entries past a device's count name valid blocks and are ignored; some device has all 32 slots live in every draw.
All inputs are finite; a program needn't handle non-finite values.
Results may differ from a plain program's by a relative error of at most 0.0065.
Values may be sent and summed in bfloat16 or wider, within the bound.
A program may use at most 128 MiB of HBM per device.

v0:
```python
import jax
import jax.numpy as jnp
from jax import lax
from jax.sharding import PartitionSpec as P

BLK = 128


def local(tokens, enc_weight, enc_bias, dec_weight, dec_bias, slot_token, slot_latent, slot_count):
    block_size = BLK
    gathered = lax.all_gather(tokens, "dp", axis=0, tiled=True)
    total_rows = gathered.shape[0]
    features = tokens.shape[1]
    capacity = slot_token.shape[0]
    live_count = slot_count[0]

    def forward_slot(slot_index, carried):
        activations, partial_value = carried
        row_start = slot_token[slot_index] * block_size
        col_start = slot_latent[slot_index] * block_size
        tok_rows = lax.dynamic_slice_in_dim(gathered, row_start, block_size, 0)
        enc_block = lax.dynamic_slice_in_dim(enc_weight, col_start, block_size, 1)
        bias_block = lax.dynamic_slice_in_dim(enc_bias, col_start, block_size, 0)
        active = (
            jnp.dot(tok_rows, enc_block, preferred_element_type=jnp.float32) + bias_block[None, :]
        ).astype(jnp.bfloat16)
        dec_block = lax.dynamic_slice_in_dim(dec_weight, col_start, block_size, 0)
        contrib = jnp.dot(active, dec_block, preferred_element_type=jnp.float32)
        previous = lax.dynamic_slice_in_dim(partial_value, row_start, block_size, 0)
        partial_value = lax.dynamic_update_slice_in_dim(
            partial_value, previous + contrib, row_start, 0
        )
        activations = lax.dynamic_update_index_in_dim(activations, active, slot_index, 0)
        return (activations, partial_value)

    empty_acts = jnp.zeros((capacity, block_size, block_size), jnp.bfloat16)
    empty_sum = jnp.zeros((total_rows, features), jnp.float32)
    activations, partial_value = lax.fori_loop(0, live_count, forward_slot, (empty_acts, empty_sum))
    share = lax.psum_scatter(partial_value, ("dp", "latent"), scatter_dimension=0, tiled=True)
    share_rows = share.shape[0]
    offset = lax.axis_index("latent") * share_rows
    token_share = lax.dynamic_slice_in_dim(tokens, offset, share_rows, 0)
    residual = share + dec_bias[None, :] - token_share.astype(jnp.float32)
    scaled = residual * 0.25
    squared, dec_bias_grad = lax.psum(
        (jnp.sum(residual * residual), jnp.sum(scaled, axis=0)), ("dp", "latent")
    )
    grad_all = lax.all_gather(scaled.astype(jnp.bfloat16), ("dp", "latent"), axis=0, tiled=True)
    mean_error = squared / (total_rows * features)

    def backward_slot(slot_index, gradients):
        enc_acc, dec_acc, bias_acc = gradients
        row_start = slot_token[slot_index] * block_size
        col_start = slot_latent[slot_index] * block_size
        tok_rows = lax.dynamic_slice_in_dim(gathered, row_start, block_size, 0)
        grad_block = lax.dynamic_slice_in_dim(grad_all, row_start, block_size, 0)
        dec_block = lax.dynamic_slice_in_dim(dec_weight, col_start, block_size, 0)
        pre_grad = lax.dot_general(
            grad_block, dec_block, (((1,), (1,)), ((), ())), preferred_element_type=jnp.float32
        )
        old_bias = lax.dynamic_slice_in_dim(bias_acc, col_start, block_size, 0)
        bias_acc = lax.dynamic_update_slice_in_dim(
            bias_acc, old_bias + jnp.sum(pre_grad, axis=0), col_start, 0
        )
        pre_half = pre_grad.astype(jnp.bfloat16)
        enc_term = lax.dot_general(
            tok_rows, pre_half, (((0,), (0,)), ((), ())), preferred_element_type=jnp.float32
        )
        old_enc = lax.dynamic_slice_in_dim(enc_acc, col_start, block_size, 1)
        enc_acc = lax.dynamic_update_slice_in_dim(enc_acc, old_enc + enc_term, col_start, 1)
        dec_term = lax.dot_general(
            activations[slot_index],
            grad_block,
            (((0,), (0,)), ((), ())),
            preferred_element_type=jnp.float32,
        )
        old_dec = lax.dynamic_slice_in_dim(dec_acc, col_start, block_size, 0)
        dec_acc = lax.dynamic_update_slice_in_dim(dec_acc, old_dec + dec_term, col_start, 0)
        return (enc_acc, dec_acc, bias_acc)

    latents_here = enc_weight.shape[1]
    start_grads = (
        jnp.zeros((features, latents_here), jnp.float32),
        jnp.zeros((latents_here, features), jnp.float32),
        jnp.zeros((latents_here,), jnp.float32),
    )
    enc_acc, dec_acc, bias_acc = lax.fori_loop(0, live_count, backward_slot, start_grads)
    return (
        enc_acc.astype(jnp.bfloat16),
        dec_acc.astype(jnp.bfloat16),
        bias_acc,
        dec_bias_grad,
        mean_error,
    )


def solution(mesh):
    in_specs = (
        P("dp", None),
        P(None, ("dp", "latent")),
        P(("dp", "latent")),
        P(("dp", "latent"), None),
        P(),
        P(("dp", "latent")),
        P(("dp", "latent")),
        P(("dp", "latent")),
    )
    out_specs = (
        P(None, ("dp", "latent")),
        P(("dp", "latent"), None),
        P(("dp", "latent")),
        P(),
        P(),
    )
    return jax.shard_map(local, mesh=mesh, in_specs=in_specs, out_specs=out_specs, check_vma=False)
```

profile of v0, /device:TPU:7, one launch (start us, length us, event | category | flops | bytes accessed | tf_op | source)
XLA Modules:
  0.0 829.1 jit_solution(1080155368049432398)
XLA Ops:
  8.0 60.8 %all-gather.3.cloned.1.call-done = bf16[1024,1536]{1,0:T(8,128)(2,1)} async-done(((bf16[128,1536]{1,0:T(8,128)(2,1)}), bf16[1024,1536]{1,0:T(8,128)(2,1)}) %all-gather.3.cloned.1.call-update) | async-done | bytes 3145744 | tf_op jit(solution)/shard_map/all_gather | solution.py:11
  69.0 3.4 broadcast.5.clone
  72.4 247.6 %while.26 = (s32[]{:T(128)}, bf16[32,128,128]{2,1,0:T(8,128)(2,1)S(1)}, f32[1024,1536]{1,0:T(8,128)}, s32[]{:T(128)}, s32[32]{0:T(128)S(1)}, /*index=5*/bf16[102...) while((s32[]{:T(128)}, ...), condition=%wide.region_1.2_spmd, body=%wide.region_0.1_spmd.sunk | while | flops 100892688 | bytes 2852675 | solution.py:38
  320.1 114.0 %reduce-scatter.2.cloned.1.call-done = f32[32,1536]{1,0:T(8,128)} async-done(((f32[1024,1536]{1,0:T(8,128)}), f32[32,1536]{1,0:T(8,128)}) %reduce-scatter.2.cloned.1.call-update) | async-done | bytes 196624 | tf_op jit(solution)/shard_map/reduce_scatter | solution.py:39
  436.3 41.5 %all-reduce = (f32[1536]{0:T(1024)}, f32[]{:T(128)}) all-reduce(f32[1536]{0:T(1024)S(1)} %get-tuple-element.125, f32[]{:T(128)} %get-tuple-element.124), channel_id=1, replica_groups=mesh['dp'=8,'latent'=4] {'dp','latent'}, use_global_device_ids=true, to_apply=%region_7.8 | all-reduce | flops 1537 | bytes 12296 | tf_op jit(solution)/shard_map/psum | solution.py:45
  478.5 18.6 %all-gather.5.cloned.1.call-done = bf16[1024,1536]{1,0:T(8,128)(2,1)} async-done(((bf16[32,1536]{1,0:T(8,128)(2,1)}), bf16[1024,1536]{1,0:T(8,128)(2,1)}) %all-gather.5.cloned.1.call-update) | async-done | bytes 3145744 | tf_op jit(solution)/shard_map/all_gather | solution.py:48
  497.2 3.4 broadcast.5
  500.6 3.4 broadcast_in_dim.15
  504.0 310.2 %while.27 = (s32[]{:T(128)}, f32[1536,1024]{1,0:T(8,128)}, f32[1024,1536]{1,0:T(8,128)}, f32[1024]{0:T(1024)S(1)}, s32[]{:T(128)}, /*index=5*/s32[32]{0:T(128)S(...) while((s32[]{:T(128)}, f32[1536,1024]{1,0:T(8,128)}, ...), condition=%wide.region_5.6_spmd, body=%wide.region_3.0_spmd.sunk | while | flops 151420944 | bytes 4819283 | solution.py:87
  508.8 2.5 fusion.41
  511.3 2.5 fusion.42
  518.5 2.5 fusion.41
  528.2 2.5 fusion.41
  537.9 2.5 fusion.41
  540.4 2.4 fusion.42
  547.5 2.5 fusion.41
  550.0 2.5 fusion.42
  557.3 2.5 fusion.41
  559.8 2.5 fusion.42
  567.0 2.5 fusion.41
  569.5 2.4 fusion.42
  576.7 2.5 fusion.41
  579.2 2.5 fusion.42
  586.4 2.5 fusion.41
  588.8 2.5 fusion.42
  596.0 2.5 fusion.41
  598.5 2.5 fusion.42
  605.7 2.5 fusion.41
  608.2 2.4 fusion.42
  615.4 2.5 fusion.41
  617.8 2.5 fusion.42
  625.0 2.5 fusion.41
  627.5 2.5 fusion.42
  634.7 2.5 fusion.41
  644.3 2.5 fusion.41
  654.0 2.5 fusion.41
  656.5 2.4 fusion.42
  663.6 2.5 fusion.41
  673.3 2.5 fusion.41
  675.8 2.5 fusion.42
  683.0 2.5 fusion.41
  685.4 2.5 fusion.42
  692.6 2.5 fusion.41
  695.1 2.5 fusion.42
  702.4 2.5 fusion.41
  712.0 2.5 fusion.41
  714.5 2.5 fusion.42
  721.7 2.5 fusion.41
  724.1 2.5 fusion.42
  731.4 2.5 fusion.41
  733.9 2.5 fusion.42
  741.1 2.5 fusion.41
  750.7 2.5 fusion.41
  760.4 2.5 fusion.41
  762.9 2.5 fusion.42
  770.1 2.5 fusion.41
  772.5 2.5 fusion.42
  779.7 2.5 fusion.41
  789.4 2.5 fusion.41
  799.0 2.5 fusion.41
  801.5 2.5 fusion.42
  808.7 2.5 fusion.41
  811.1 2.5 fusion.42
  814.3 5.1 convert_element_type.20
  (318 shorter events, 301.2 us)
Async XLA Ops:
  7.2 65.2 %copy-start.3 = (s32[32]{0:T(128)S(1)}, s32[32]{0:T(128)}, u32[]{:S(2)}) copy-start(s32[32]{0:T(128)} %param.18) | copy-start | bytes 388
  7.2 65.2 %copy-start.4 = (s32[32]{0:T(128)S(1)}, s32[32]{0:T(128)}, u32[]{:S(2)}) copy-start(s32[32]{0:T(128)} %param.17) | copy-start | bytes 388
  7.2 61.5 %all-gather.3.cloned.1.call-start = ((), (), s32[]{:S(2)}) async-start(), calls=%async_computation.1 | async-start | bytes 3538944 | tf_op jit(solution)/shard_map/all_gather | solution.py:11
  7.9 426.1 %reduce-scatter.2.cloned.1.call-start = ((), (), s32[]{:S(2)}) async-start(), calls=%async_computation.2 | async-start | bytes 6488064 | tf_op jit(solution)/shard_map/reduce_scatter | solution.py:39
  320.0 114.1 %copy-start.2 = (f32[1536]{0:T(1024)S(1)}, f32[1536]{0:T(1024)}, u32[]{:S(2)}) copy-start(f32[1536]{0:T(1024)} %param.16) | copy-start | bytes 18436
  320.0 177.2 %all-gather.5.cloned.1.call-start = ((), (), s32[]{:S(2)}) async-start(), calls=%async_computation.3 | async-start | bytes 3244032 | tf_op jit(solution)/shard_map/all_gather | solution.py:48
  814.2 7.2 copy-start.1
  814.3 5.1 copy-start
Sparse Core Ops, SparseCore 0:
  10.2 58.5 all-gather.2
  320.1 113.8 reduce-scatter.1
  437.5 59.6 all-gather.4
where the time goes:
time: 836 us; the launch traced here: 829 us
  matrix products  324 us (39%)
  waiting for transfers between devices  194 us (23%)
  loops' own time  128 us (15%)
  local copies, waits for them, and re-layouts  110 us (13%)
  blocking collectives  41.5 us (5%)
  between operations  15.6 us (2%)
  other arithmetic  15.4 us (2%)
    reduce_scatter x1, waiting for transfers between devices, local(): lax.psum_scatter(partial_value, ('dp', 'latent'), scatter_dimension=0, ti...  114 us
    dot_general x32, matrix products, backward_slot(): lax.dot_general(tok_rows, pre_half, (((0,), (0,)), ((), ())), preferred_e...  79.5 us
    dot_general x32, matrix products, backward_slot(): lax.dot_general(activations[slot_index], grad_block, (((0,), (0,)), ((),...  78.3 us
    dot_general x32, matrix products, forward_slot(): contrib = jnp.dot(active, dec_block, preferred_element_type=jnp.float32)  77.1 us
    another operation x1, loops' own time, local(): lax.fori_loop(0, live_count, backward_slot, start_grads)  64.1 us
    another operation x1, loops' own time, local(): lax.fori_loop(0, live_count, forward_slot, (empty_acts, empty_sum))  64.1 us
    all_gather x1, waiting for transfers between devices, local(): gathered = lax.all_gather(tokens, 'dp', axis=0, tiled=True)  60.8 us
    dot_general x32, matrix products, backward_slot(): lax.dot_general(grad_block, dec_block, (((1,), (1,)), ((), ())), preferre...  44.6 us
  transfers between devices with their start and end apart: 3, of which 3 were waited for; matrix products, arithmetic and copies ran while one was open for 0% of the time, Pallas kernels for 0%

commit v1 on v0

--- a/solution.py
+++ b/solution.py
@@ -8,7 +8,14 @@
 
 def local(tokens, enc_weight, enc_bias, dec_weight, dec_bias, slot_token, slot_latent, slot_count):
     block_size = BLK
-    gathered = lax.all_gather(tokens, "dp", axis=0, tiled=True)
+    peers = lax.axis_size("dp")
+    hops = [(i, (i + 1) % peers) for i in range(peers)]
+    parts = [tokens]
+    for reach in range(1, peers):
+        parts = [lax.ppermute(parts[0], "dp", hops), *parts]
+    whole = jnp.concatenate(parts, axis=0)
+    turn = (lax.axis_index("dp") + 1) * parts[-1].shape[0]
+    gathered = jnp.roll(whole, turn, axis=0)
     total_rows = gathered.shape[0]
     features = tokens.shape[1]
     capacity = slot_token.shape[0]

time: 836 us -> 863 us (1.032)
  matrix products: 324 us -> 336 us
    ppermute x0 -> x7, waiting for transfers between devices: none -> 66.2 us  [local(): parts = [lax.ppermute(parts[0], 'dp', hops), *parts]]
    all_gather x1 -> x0, waiting for transfers between devices: 60.8 us -> none  [local(): gathered = lax.all_gather(tokens, 'dp', axis=0, tiled=True)]
    dot_general x32, matrix products: 44.2 us -> 59.7 us  [forward_slot(): jnp.dot(tok_rows, enc_block, preferred_element_type=jnp.float32)]
  transfers between devices with their start and end apart: 3 -> 9, of which waited for: 3 -> 9; matrix products, arithmetic and copies ran while one was open for 0% -> 0% of each run, Pallas kernels for 0% -> 0%
where the time goes in v1:
time: 863 us; the launch traced here: 855 us
  matrix products  336 us (39%)
  waiting for transfers between devices  200 us (23%)
  loops' own time  128 us (15%)
  local copies, waits for them, and re-layouts  113 us (13%)
  blocking collectives  41.5 us (5%)
  between operations  16 us (2%)
  other arithmetic  15.3 us (2%)
    reduce_scatter x1, waiting for transfers between devices, local(): lax.psum_scatter(partial_value, ('dp', 'latent'), scatter_dimension=0, ti...  115 us
    dot_general x32, matrix products, backward_slot(): lax.dot_general(activations[slot_index], grad_block, (((0,), (0,)), ((),...  78.9 us
    dot_general x32, matrix products, forward_slot(): contrib = jnp.dot(active, dec_block, preferred_element_type=jnp.float32)  76.9 us
    dot_general x32, matrix products, backward_slot(): lax.dot_general(tok_rows, pre_half, (((0,), (0,)), ((), ())), preferred_e...  76.2 us
    ppermute x7, waiting for transfers between devices, local(): parts = [lax.ppermute(parts[0], 'dp', hops), *parts]  66.2 us
    another operation x1, loops' own time, local(): lax.fori_loop(0, live_count, backward_slot, start_grads)  64.1 us
    another operation x1, loops' own time, local(): lax.fori_loop(0, live_count, forward_slot, (empty_acts, empty_sum))  64.1 us
    dot_general x32, matrix products, forward_slot(): jnp.dot(tok_rows, enc_block, preferred_element_type=jnp.float32)  59.7 us
  transfers between devices with their start and end apart: 9, of which 9 were waited for; matrix products, arithmetic and copies ran while one was open for 0% of the time, Pallas kernels for 0%

profile of v1, /device:TPU:7, one launch (start us, length us, event | category | flops | bytes accessed | tf_op | source)
XLA Modules:
  0.0 854.9 jit_solution(1532430630030133414)
XLA Ops:
  8.5 8.9 %collective-permute-done = bf16[128,1536]{1,0:T(8,128)(2,1)S(1)} collective-permute-done((bf16[128,1536]{1,0:T(8,128)(2,1)}, bf16[128,1536]{1,0:T(8,128)(2,1)S(1)}, u32[]{:S(2)}, u32[]{:S(2)}) %collective-permute-start) | collective-permute-done | bytes 393248 | tf_op jit(solution)/shard_map/ppermute | solution.py:15
  19.7 9.0 %collective-permute-done.1 = bf16[128,1536]{1,0:T(8,128)(2,1)S(1)} collective-permute-done((bf16[128,1536]{1,0:T(8,128)(2,1)S(1)}, bf16[128,1536]{1,0:T(8,128)(2,1)S(1)}, u32[]{:S(2)}, u32[]{:S(2)}) %collective-permute-start.1) | collective-permute-done | bytes 393248 | tf_op jit(solution)/shard_map/ppermute | solution.py:15
  29.7 10.1 %collective-permute-done.2 = bf16[128,1536]{1,0:T(8,128)(2,1)S(1)} collective-permute-done((bf16[128,1536]{1,0:T(8,128)(2,1)S(1)}, bf16[128,1536]{1,0:T(8,128)(2,1)S(1)}, u32[]{:S(2)}, u32[]{:S(2)}) %collective-permute-start.2) | collective-permute-done | bytes 393248 | tf_op jit(solution)/shard_map/ppermute | solution.py:15
  39.8 10.2 %collective-permute-done.3 = bf16[128,1536]{1,0:T(8,128)(2,1)S(1)} collective-permute-done((bf16[128,1536]{1,0:T(8,128)(2,1)S(1)}, bf16[128,1536]{1,0:T(8,128)(2,1)S(1)}, u32[]{:S(2)}, u32[]{:S(2)}) %collective-permute-start.3) | collective-permute-done | bytes 393248 | tf_op jit(solution)/shard_map/ppermute | solution.py:15
  50.0 9.4 %collective-permute-done.4 = bf16[128,1536]{1,0:T(8,128)(2,1)S(1)} collective-permute-done((bf16[128,1536]{1,0:T(8,128)(2,1)S(1)}, bf16[128,1536]{1,0:T(8,128)(2,1)S(1)}, u32[]{:S(2)}, u32[]{:S(2)}) %collective-permute-start.4) | collective-permute-done | bytes 393248 | tf_op jit(solution)/shard_map/ppermute | solution.py:15
  59.3 9.0 %collective-permute-done.5 = bf16[128,1536]{1,0:T(8,128)(2,1)S(1)} collective-permute-done((bf16[128,1536]{1,0:T(8,128)(2,1)S(1)}, bf16[128,1536]{1,0:T(8,128)(2,1)S(1)}, u32[]{:S(2)}, u32[]{:S(2)}) %collective-permute-start.5) | collective-permute-done | bytes 393248 | tf_op jit(solution)/shard_map/ppermute | solution.py:15
  68.4 9.5 %collective-permute-done.6 = bf16[128,1536]{1,0:T(8,128)(2,1)S(1)} collective-permute-done((bf16[128,1536]{1,0:T(8,128)(2,1)S(1)}, bf16[128,1536]{1,0:T(8,128)(2,1)S(1)}, u32[]{:S(2)}, u32[]{:S(2)}) %collective-permute-start.6) | collective-permute-done | bytes 393248 | tf_op jit(solution)/shard_map/ppermute | solution.py:15
  80.9 3.4 broadcast.6.clone
  84.4 262.8 %while.26 = (s32[]{:T(128)}, bf16[32,128,128]{2,1,0:T(8,128)(2,1)}, f32[1024,1536]{1,0:T(8,128)}, s32[]{:T(128)}, s32[32]{0:T(128)S(1)}, /*index=5*/bf16[1024,15...) while((s32[]{:T(128)}, bf16[32,128,128]{2,1,0:T(8,128)(2,1)}, ...), condition=%wide.region_1.2_spmd, body=%wide.region_0.1_spmd.sunk | while | flops 100892688 | bytes 2852675 | solution.py:45
  98.3 2.4 fusion.35
  106.6 2.4 fusion.35
  122.9 2.4 fusion.35
  131.1 2.4 fusion.35
  155.7 2.4 fusion.35
  180.3 2.4 fusion.35
  196.7 2.4 fusion.35
  213.1 2.4 fusion.35
  229.4 2.4 fusion.35
  262.2 2.4 fusion.35
  270.4 2.4 fusion.35
  347.2 115.1 %reduce-scatter.2.cloned.1.call-done = f32[32,1536]{1,0:T(8,128)} async-done(((f32[1024,1536]{1,0:T(8,128)}), f32[32,1536]{1,0:T(8,128)}) %reduce-scatter.2.cloned.1.call-update) | async-done | bytes 196624 | tf_op jit(solution)/shard_map/reduce_scatter | solution.py:46
  464.5 41.5 %all-reduce = (f32[1536]{0:T(1024)}, f32[]{:T(128)}) all-reduce(f32[1536]{0:T(1024)S(1)} %get-tuple-element.125, f32[]{:T(128)} %get-tuple-element.124), channel_id=1, replica_groups=mesh['dp'=8,'latent'=4] {'dp','latent'}, use_global_device_ids=true, to_apply=%region_7.8 | all-reduce | flops 1537 | bytes 12296 | tf_op jit(solution)/shard_map/psum | solution.py:52
  506.7 18.7 %all-gather.2.cloned.1.call-done = bf16[1024,1536]{1,0:T(8,128)(2,1)} async-done(((bf16[32,1536]{1,0:T(8,128)(2,1)}), bf16[1024,1536]{1,0:T(8,128)(2,1)}) %all-gather.2.cloned.1.call-update) | async-done | bytes 3145744 | tf_op jit(solution)/shard_map/all_gather | solution.py:55
  525.4 3.4 broadcast.6
  528.8 3.4 broadcast_in_dim.15
  532.3 307.5 %while.27 = (s32[]{:T(128)}, f32[1536,1024]{1,0:T(8,128)}, f32[1024,1536]{1,0:T(8,128)}, f32[1024]{0:T(1024)S(1)}, s32[]{:T(128)}, /*index=5*/s32[32]{0:T(128)S(...) while((s32[]{:T(128)}, f32[1536,1024]{1,0:T(8,128)}, ...), condition=%wide.region_5.6_spmd, body=%wide.region_3.5_spmd.sunk | while | flops 151420944 | bytes 4819283 | solution.py:94
  539.4 2.5 fusion.42
  549.0 2.5 fusion.42
  558.6 2.5 fusion.42
  568.2 2.4 fusion.42
  577.7 2.5 fusion.42
  587.3 2.5 fusion.42
  597.0 2.4 fusion.42
  606.5 2.5 fusion.42
  613.7 2.4 fusion.41
  616.1 2.5 fusion.42
  625.7 2.5 fusion.42
  635.3 2.5 fusion.42
  642.5 2.4 fusion.41
  644.9 2.5 fusion.42
  652.1 2.4 fusion.41
  654.5 2.5 fusion.42
  664.1 2.4 fusion.42
  673.6 2.5 fusion.42
  683.2 2.4 fusion.42
  692.7 2.5 fusion.42
  702.3 2.5 fusion.42
  711.9 2.5 fusion.42
  721.5 2.5 fusion.42
  731.2 2.4 fusion.42
  738.3 2.4 fusion.41
  740.8 2.5 fusion.42
  750.3 2.5 fusion.42
  760.0 2.5 fusion.42
  769.6 2.4 fusion.42
  779.2 2.5 fusion.42
  788.7 2.5 fusion.42
  795.9 2.4 fusion.41
  798.3 2.5 fusion.42
  807.9 2.5 fusion.42
  817.5 2.4 fusion.42
  827.0 2.5 fusion.42
  836.6 2.5 fusion.42
  839.8 5.1 convert_element_type.20
  (352 shorter events, 336.2 us)
Async XLA Ops:
  7.2 72.3 %copy-start.1 = (bf16[128,1536]{1,0:T(8,128)(2,1)S(1)}, bf16[128,1536]{1,0:T(8,128)(2,1)}, u32[]{:S(2)}) copy-start(bf16[128,1536]{1,0:T(8,128)(2,1)} %param.12) | copy-start | bytes 1179652
  7.2 455.1 %reduce-scatter.2.cloned.1.call-start = ((), (), s32[]{:S(2)}) async-start(), calls=%async_computation.1 | async-start | bytes 6488064 | tf_op jit(solution)/shard_map/reduce_scatter | solution.py:46
  7.2 10.3 %collective-permute-start = (bf16[128,1536]{1,0:T(8,128)(2,1)}, bf16[128,1536]{1,0:T(8,128)(2,1)S(1)}, u32[]{:S(2)}, u32[]{:S(2)}) collective-permute-start(bf16[128,1536]{1,0:T(8,128)(2,1)} %param.12), channel_id=1, source_target_pairs={{0,4},{4,8},{8,12},{12,16},{16,20},{20,24},{24,28},{28,0},{1,5},{5... | collective-permute-start | bytes 1179656 | tf_op jit(solution)/shard_map/ppermute | solution.py:15
  17.5 11.2 %collective-permute-start.1 = (bf16[128,1536]{1,0:T(8,128)(2,1)S(1)}, bf16[128,1536]{1,0:T(8,128)(2,1)S(1)}, u32[]{:S(2)}, u32[]{:S(2)}) collective-permute-start(bf16[128,1536]{1,0:T(8,128)(2,1)S(1)} %collective-permute-done), channel_id=1, source_target_pairs={{0,4},{4,8},{8,12},{12,16},{16,20},{20,24},{24,28},{28,0},{1,5},{5... | collective-permute-start | bytes 1179656 | tf_op jit(solution)/shard_map/ppermute | solution.py:15
  28.7 11.1 %collective-permute-start.2 = (bf16[128,1536]{1,0:T(8,128)(2,1)S(1)}, bf16[128,1536]{1,0:T(8,128)(2,1)S(1)}, u32[]{:S(2)}, u32[]{:S(2)}) collective-permute-start(bf16[128,1536]{1,0:T(8,128)(2,1)S(1)} %collective-permute-done.1), channel_id=1, source_target_pairs={{0,4},{4,8},{8,12},{12,16},{16,20},{20,24},{24,28},{28,0},{1,5},{5... | collective-permute-start | bytes 1179656 | tf_op jit(solution)/shard_map/ppermute | solution.py:15
  39.8 10.2 %collective-permute-start.3 = (bf16[128,1536]{1,0:T(8,128)(2,1)S(1)}, bf16[128,1536]{1,0:T(8,128)(2,1)S(1)}, u32[]{:S(2)}, u32[]{:S(2)}) collective-permute-start(bf16[128,1536]{1,0:T(8,128)(2,1)S(1)} %collective-permute-done.2), channel_id=1, source_target_pairs={{0,4},{4,8},{8,12},{12,16},{16,20},{20,24},{24,28},{28,0},{1,5},{5... | collective-permute-start | bytes 1179656 | tf_op jit(solution)/shard_map/ppermute | solution.py:15
  50.0 9.4 %collective-permute-start.4 = (bf16[128,1536]{1,0:T(8,128)(2,1)S(1)}, bf16[128,1536]{1,0:T(8,128)(2,1)S(1)}, u32[]{:S(2)}, u32[]{:S(2)}) collective-permute-start(bf16[128,1536]{1,0:T(8,128)(2,1)S(1)} %collective-permute-done.3), channel_id=1, source_target_pairs={{0,4},{4,8},{8,12},{12,16},{16,20},{20,24},{24,28},{28,0},{1,5},{5... | collective-permute-start | bytes 1179656 | tf_op jit(solution)/shard_map/ppermute | solution.py:15
  59.3 9.0 %collective-permute-start.5 = (bf16[128,1536]{1,0:T(8,128)(2,1)S(1)}, bf16[128,1536]{1,0:T(8,128)(2,1)S(1)}, u32[]{:S(2)}, u32[]{:S(2)}) collective-permute-start(bf16[128,1536]{1,0:T(8,128)(2,1)S(1)} %collective-permute-done.4), channel_id=1, source_target_pairs={{0,4},{4,8},{8,12},{12,16},{16,20},{20,24},{24,28},{28,0},{1,5},{5... | collective-permute-start | bytes 1179656 | tf_op jit(solution)/shard_map/ppermute | solution.py:15
  68.3 9.5 %collective-permute-start.6 = (bf16[128,1536]{1,0:T(8,128)(2,1)S(1)}, bf16[128,1536]{1,0:T(8,128)(2,1)S(1)}, u32[]{:S(2)}, u32[]{:S(2)}) collective-permute-start(bf16[128,1536]{1,0:T(8,128)(2,1)S(1)} %collective-permute-done.5), channel_id=1, source_target_pairs={{0,4},{4,8},{8,12},{12,16},{16,20},{20,24},{24,28},{28,0},{1,5},{5... | collective-permute-start | bytes 1179656 | tf_op jit(solution)/shard_map/ppermute | solution.py:15
  79.5 4.9 copy-start.4
  79.5 4.9 copy-start.6
  347.1 115.2 %copy-start.3 = (f32[1536]{0:T(1024)S(1)}, f32[1536]{0:T(1024)}, u32[]{:S(2)}) copy-start(f32[1536]{0:T(1024)} %param.16) | copy-start | bytes 18436
  347.2 178.2 %all-gather.2.cloned.1.call-start = ((), (), s32[]{:S(2)}) async-start(), calls=%async_computation.2 | async-start | bytes 3244032 | tf_op jit(solution)/shard_map/all_gather | solution.py:55
  525.4 6.9 copy-start.5
  525.4 6.9 copy-start.7
  839.8 7.2 copy-start.2
  839.8 5.1 copy-start
Sparse Core Ops, SparseCore 0:
  347.3 114.9 reduce-scatter.1
  465.8 59.6 all-gather.1
